TPU v7x, 32 devices: a whole 2x2x4 slice. The times are simulated.
32 devices in a mesh: clip: 2 (over y), tm: 4 (over z), band: 2 (over x), head: 2 (over core).
Axes of the slice: x: 2, y: 2, z: 4, core: 2. Of those that a mesh axis runs over, the one named last changes fastest.
Arguments:
- queries: bfloat16 [8, 2, 256, 1536], P(('clip', 'tm'), 'band', None, 'head'), parts along dimension 0, may hold values from -6 to 6
- keys: bfloat16 [8, 2, 256, 1536], P(('clip', 'tm'), 'band', None, 'head'), parts along dimension 0, may hold values from -6 to 6
- values: bfloat16 [8, 2, 256, 1536], P(('clip', 'tm'), 'band', None, 'head'), parts along dimension 0, may hold values from -6 to 6
- adj_mask: int32 [8, 2, 2, 2], P(('clip', 'tm'), 'band'), parts along dimension 0, may hold values from 0 to 1, as said below
- border_blocks: int32 [8, 2, 2, 1], P(('clip', 'tm'), 'band'), parts along dimension 0, may hold values from 0 to 1
Outputs:
- attended: bfloat16 [8, 2, 256, 1536], P(('clip', 'tm'), 'band', None, 'head'), parts along dimension 0
There are 2 independent parts, one for each index of `clip`. A program takes and returns all parts, laid end to end along the dimension named above; each array names one. Nothing has to cross between parts.
Inputs may be any that keep to these rules, and one draw needn't show every extreme that they name: `adj_mask`: for each slab, band and direction exactly 1 of the 2 entries are 1.
All inputs are finite; a program needn't handle non-finite values.
Results may differ from a plain program's by a relative error of at most 0.0043.
Values may be sent and summed in bfloat16 or wider, within the bound.
A program may use at most 64 MiB of HBM per device.

v0:
```python
import functools
import math

import jax
import jax.numpy as jnp
from jax import lax
from jax.experimental import pallas as pl
from jax.experimental.pallas import tpu as pltpu
from jax.sharding import PartitionSpec as P

BLK = 128
HD = 128

masked_score = -1e30
SCALE2 = math.log2(math.e) / math.sqrt(HD)
MESH = pl.DeviceIdType.MESH


def routes(slab_count, band_count):
    slab, band = lax.axis_index("tm"), lax.axis_index("band")
    found = []
    if slab_count > 1:
        found.append(({"tm": slab + 1}, slab < slab_count - 1, None, slab > 0, ("adj", 0)))
        found.append(({"tm": slab - 1}, None, slab > 0, slab < slab_count - 1, ("adj", 1)))
    if band_count == 2:
        found.append(({"band": 1 - band}, band == 0, band == 1, None, ("border", 1 - band)))
    elif band_count > 2:
        found.append(({"band": band + 1}, band < band_count - 1, None, band > 0, ("border", 1)))
        found.append(({"band": band - 1}, None, band > 0, band < band_count - 1, ("border", 0)))
    return found


def when(condition):
    return (lambda body: body()) if condition is None else pl.when(condition)


def chunks_of(heads):
    return (
        [(0, heads)],
        [(0, heads - 1), (heads - 1, 1)],
    )


def weigh(query, key):
    scores = lax.dot_general(
        query, key, (((1,), (1,)), ((), ())), preferred_element_type=jnp.float32
    )
    return scores * SCALE2


def kernel(
    slab_count, band_count, q_hbm, k_hbm, v_hbm, adj_hbm, border_hbm, out_ref,
    q_ref, k_ref, v_ref, adj_ref, border_ref, send_ref, recv_ref, acc_ref, weights_ref,
    gain_ref, load_sem, here_sem, send_sem, recv_sem,
):
    plan = routes(slab_count, band_count)
    rows, width = q_ref.shape
    heads = width // HD

    neighbours = []
    for axis, count in (("tm", slab_count), ("band", band_count)):
        if count > 1:
            index = lax.axis_index(axis)
            neighbours.append((axis, index, index > 0, index < count - 1))

    barrier = pltpu.get_barrier_semaphore()
    for axis, index, _, has_upper in neighbours:
        @pl.when(has_upper)
        def _():
            pl.semaphore_signal(barrier, inc=1, device_id={axis: index + 1}, device_id_type=MESH)

    picks = []
    for number, (source, target) in enumerate(((adj_hbm, adj_ref), (border_hbm, border_ref))):
        picks.append(pltpu.make_async_copy(source, target, load_sem.at[number]))
    for pick in picks:
        pick.start()
    loads = [
        pltpu.make_async_copy(source, target, load_sem.at[2 + number])
        for number, (source, target) in enumerate(((k_hbm, k_ref), (v_hbm, v_ref), (q_hbm, q_ref)))
    ]
    loads[0].start()

    chunks = chunks_of(heads)

    def transfer(slot, part, group):
        at = (slot, part, pl.ds(*chunks[part][group]))
        return pltpu.make_async_remote_copy(
            src_ref=send_ref.at[at],
            dst_ref=recv_ref.at[at],
            send_sem=send_sem.at[slot, part, group],
            recv_sem=recv_sem.at[slot, part, group],
            device_id=plan[slot][0],
            device_id_type=MESH,
        )

    def send(part, downward):
        for group in range(len(chunks[part])):
            for slot, (_, up, down, _, _) in enumerate(plan):
                sends = down if downward else up
                if sends is not None:
                    @pl.when(sends)
                    def _():
                        transfer(slot, part, group).start()

    arrivals = sum(lower.astype(jnp.int32) for _, _, lower, _ in neighbours)

    @pl.when(arrivals > 0)
    def _():
        pl.semaphore_wait(barrier, arrivals)

    for number, (axis, index, has_lower, _) in enumerate(neighbours):
        @pl.when(has_lower)
        def _():
            pl.semaphore_signal(
                here_sem.at[number], inc=1, device_id={axis: index - 1}, device_id_type=MESH
            )

    for pick in picks:
        pick.wait()
    blocks = [
        adj_ref[row, 1] if kind == "adj" else border_ref[0, row] for _, _, _, _, (kind, row) in plan
    ]
    for part, whole in enumerate((k_ref, v_ref)):
        loads[part].wait()
        if part == 0:
            loads[1].start()
            loads[2].start()
        for slot in range(len(plan)):
            for head in range(heads):
                send_ref[slot, part, head] = whole[blocks[slot], :, head * HD : (head + 1) * HD]
        send(part, True)
    for number, (_, _, _, has_upper) in enumerate(neighbours):
        @pl.when(has_upper)
        def _():
            pl.semaphore_wait(here_sem.at[number], 1)
    for part in range(2):
        send(part, False)

    for slot, (_, _, _, comes, _) in enumerate(plan):
        if comes is not None:
            @pl.when(jnp.logical_not(comes))
            def _():
                recv_ref[slot] = jnp.zeros(recv_ref.shape[1:], recv_ref.dtype)

    loads[2].wait()
    own = []
    for head in range(heads):
        columns = slice(head * HD, (head + 1) * HD)
        scores = weigh(q_ref[:, columns], k_ref[:, :, columns].reshape(rows, HD))
        most = jnp.max(scores, axis=1, keepdims=True)
        weights = jnp.exp2(scores - most)
        total = jnp.sum(weights, axis=1, keepdims=True)
        acc_ref[head] = jnp.dot(
            weights.astype(jnp.bfloat16), v_ref[:, :, columns].reshape(rows, HD), preferred_element_type=jnp.float32
        )
        own.append((most, total))

    for group, (start, size) in enumerate(chunks[0]):
        for slot, (_, _, _, comes, _) in enumerate(plan):
            @when(comes)
            def _():
                transfer(slot, 0, group).wait_recv()
        for head in range(start, start + size):
            columns = slice(head * HD, (head + 1) * HD)
            pieces = [own[head]]
            for slot, (_, _, _, comes, _) in enumerate(plan):
                scores = weigh(q_ref[:, columns], recv_ref[slot, 0, head])
                if comes is not None:
                    scores = scores + jnp.where(comes, 0.0, masked_score).astype(jnp.float32)
                most = jnp.max(scores, axis=1, keepdims=True)
                weights = jnp.exp2(scores - most)
                total = jnp.sum(weights, axis=1, keepdims=True)
                weights_ref[head, slot] = weights.astype(jnp.bfloat16)
                pieces.append((most, total))
            largest = functools.reduce(jnp.maximum, [most for most, _ in pieces])
            factors = [jnp.exp2(most - largest) for most, _ in pieces]
            denominator = sum(factor * total for factor, (_, total) in zip(factors, pieces))
            acc_ref[head] = acc_ref[head] * (factors[0] / denominator)
            for slot in range(len(plan)):
                gain_ref[head, slot] = jnp.broadcast_to(
                    factors[slot + 1] / denominator, (rows, HD)
                )

    for group, (start, size) in enumerate(chunks[1]):
        for slot, (_, _, _, comes, _) in enumerate(plan):
            @when(comes)
            def _():
                transfer(slot, 1, group).wait_recv()
        for head in range(start, start + size):
            result = acc_ref[head]
            for slot in range(len(plan)):
                result = result + gain_ref[head, slot] * jnp.dot(
                    weights_ref[head, slot], recv_ref[slot, 1, head], preferred_element_type=jnp.float32
                )
            out_ref[:, head * HD : (head + 1) * HD] = result.astype(out_ref.dtype)

    for part in range(2):
        for group in range(len(chunks[part])):
            for slot, (_, up, down, _, _) in enumerate(plan):
                sends = down if up is None else up if down is None else None

                @when(sends)
                def _():
                    transfer(slot, part, group).wait_send()


def per_device(queries, keys, values, adj_mask, border_blocks):
    rows, width = queries.shape[2:]
    heads = width // HD
    slab_count, band_count = lax.axis_size("tm"), lax.axis_size("band")
    sources = (2 if slab_count > 1 else 0) + min(band_count - 1, 2)
    assert rows == 2 * BLK and adj_mask.shape[3] == 2 and border_blocks.shape[3] == 1
    block_sems = pltpu.SemaphoreType.DMA((sources, 2, max(map(len, chunks_of(heads)))))
    attended = pl.pallas_call(
        functools.partial(kernel, slab_count, band_count),
        out_shape=pltpu.VMEM((rows, width), jnp.bfloat16),
        in_specs=[pl.BlockSpec(memory_space=pl.ANY)] * 5,
        out_specs=pl.BlockSpec(memory_space=pltpu.VMEM),
        scratch_shapes=[
            pltpu.VMEM((rows, width), jnp.bfloat16),
            pltpu.VMEM((rows // BLK, BLK, width), jnp.bfloat16),
            pltpu.VMEM((rows // BLK, BLK, width), jnp.bfloat16),
            pltpu.SMEM(adj_mask.shape[2:], jnp.int32),
            pltpu.SMEM(border_blocks.shape[:1:-1], jnp.int32),
            pltpu.VMEM((sources, 2, heads, BLK, HD), jnp.bfloat16),
            pltpu.VMEM((sources, 2, heads, BLK, HD), jnp.bfloat16),
            pltpu.VMEM((heads, rows, HD), jnp.float32),
            pltpu.VMEM((heads, sources, rows, BLK), jnp.bfloat16),
            pltpu.VMEM((heads, sources, rows, HD), jnp.float32),
            pltpu.SemaphoreType.DMA((5,)),
            pltpu.SemaphoreType.REGULAR((max(1, (slab_count > 1) + (band_count > 1)),)),
            block_sems,
            block_sems,
        ],
        compiler_params=pltpu.CompilerParams(collective_id=0, has_side_effects=True),
        name="radial_attention",
    )(
        queries[0, 0],
        keys.reshape(rows // BLK, BLK, width),
        values.reshape(rows // BLK, BLK, width),
        adj_mask[0, 0], border_blocks[0, 0].T,
    )
    return attended[None, None]


def solution(mesh):
    placed = (
        P(("clip", "tm"), "band", None, "head"),
        P(("clip", "tm"), "band", None, "head"),
        P(("clip", "tm"), "band", None, "head"),
        P(("clip", "tm"), "band", None, None),
        P(("clip", "tm"), "band", None, None),
    )
    return jax.shard_map(
        per_device,
        mesh=mesh,
        in_specs=placed,
        out_specs=P(("clip", "tm"), "band", None, "head"),
        check_vma=False,
    )
```

profile of v0, /device:TPU:0, one launch (start us, length us, event | category | flops | bytes accessed | tf_op | source)
XLA Modules:
  0.0 14.6 jit_solution(1902447765701113578)
XLA Ops:
  0.0 13.8 %radial_attention.1 = bf16[256,768]{1,0:T(8,128)(2,1)S(1)} custom-call(bf16[256,768]{1,0:T(8,128)(2,1)} %bitcast.7, bf16[2,128,768]{2,1,0:T(8,128)(2,1)} %bitcast.8, bf16[2,128,768]{2,1,0:T(8,128)(2,1)} %bitcast.9, s32[2,2]{1,0:T(2,128)} %bitcast.10, s32[1,2]{1,0:T(1,128)} %bitcast.11), custom_call_target="tpu_custom_call" | custom-call | tf_op jit(solution)/shard_map/radial_attention/pallas_call | solution.py:214
  13.8 0.7 %copy.7 = bf16[1,1,256,768]{3,2,1,0:T(8,128)(2,1)} copy(bf16[1,1,256,768]{3,2,1,0:T(8,128)(2,1)S(1)} %bitcast.6) | data formatting | bytes 786432
where the time goes:
time: 14.8 us; the launch traced here: 14.6 us
  Pallas kernels  13.8 us (93%)
  local copies, waits for them, and re-layouts  0.75 us (5%)
    pallas_call x1, Pallas kernels, per_device(): pl.pallas_call(functools.partial(kernel, slab_count, band_count), out_sha...  13.8 us
    unnamed x1, local copies, waits for them, and re-layouts  0.75 us

commit v1 on v0

--- a/solution.py
+++ b/solution.py
@@ -78,7 +78,8 @@
         pltpu.make_async_copy(source, target, load_sem.at[2 + number])
         for number, (source, target) in enumerate(((k_hbm, k_ref), (v_hbm, v_ref), (q_hbm, q_ref)))
     ]
-    loads[0].start()
+    for load in loads:
+        load.start()
 
     chunks = chunks_of(heads)
 
@@ -120,21 +121,23 @@
     blocks = [
         adj_ref[row, 1] if kind == "adj" else border_ref[0, row] for _, _, _, _, (kind, row) in plan
     ]
+    late = lax.axis_index("head") > 0
     for part, whole in enumerate((k_ref, v_ref)):
         loads[part].wait()
-        if part == 0:
-            loads[1].start()
-            loads[2].start()
         for slot in range(len(plan)):
             for head in range(heads):
                 send_ref[slot, part, head] = whole[blocks[slot], :, head * HD : (head + 1) * HD]
-        send(part, True)
-    for number, (_, _, _, has_upper) in enumerate(neighbours):
-        @pl.when(has_upper)
-        def _():
-            pl.semaphore_wait(here_sem.at[number], 1)
-    for part in range(2):
-        send(part, False)
+        if part == 0:
+            send(0, True)
+            for number, (_, _, _, has_upper) in enumerate(neighbours):
+                @pl.when(has_upper)
+                def _():
+                    pl.semaphore_wait(here_sem.at[number], 1)
+            send(0, False)
+    @pl.when(jnp.logical_not(late))
+    def _():
+        send(1, True)
+        send(1, False)
 
     for slot, (_, _, _, comes, _) in enumerate(plan):
         if comes is not None:
@@ -160,6 +163,11 @@
             @when(comes)
             def _():
                 transfer(slot, 0, group).wait_recv()
+        @pl.when(late)
+        def _():
+            send(1, True)
+            send(1, False)
+
         for head in range(start, start + size):
             columns = slice(head * HD, (head + 1) * HD)
             pieces = [own[head]]

time: 14.8 us -> 14.1 us (0.953)
  the two profiles are of different devices: /device:TPU:0 before, /device:TPU:1 now
where the time goes in v1:
time: 14.1 us; the launch traced here: 13.9 us
  Pallas kernels  13.2 us (94%)
  local copies, waits for them, and re-layouts  0.75 us (5%)
    pallas_call x1, Pallas kernels, per_device(): pl.pallas_call(functools.partial(kernel, slab_count, band_count), out_sha...  13.2 us
    unnamed x1, local copies, waits for them, and re-layouts  0.75 us

profile of v1, /device:TPU:1, one launch (start us, length us, event | category | flops | bytes accessed | tf_op | source)
XLA Modules:
  0.0 13.9 jit_solution(12772565524449066172)
XLA Ops:
  0.0 13.2 %radial_attention.1 = bf16[256,768]{1,0:T(8,128)(2,1)S(1)} custom-call(bf16[256,768]{1,0:T(8,128)(2,1)} %bitcast.7, bf16[2,128,768]{2,1,0:T(8,128)(2,1)} %bitcast.8, bf16[2,128,768]{2,1,0:T(8,128)(2,1)} %bitcast.9, s32[2,2]{1,0:T(2,128)} %bitcast.10, s32[1,2]{1,0:T(1,128)} %bitcast.11), custom_call_target="tpu_custom_call" | custom-call | tf_op jit(solution)/shard_map/radial_attention/pallas_call | solution.py:222
  13.2 0.7 %copy.7 = bf16[1,1,256,768]{3,2,1,0:T(8,128)(2,1)} copy(bf16[1,1,256,768]{3,2,1,0:T(8,128)(2,1)S(1)} %bitcast.6) | data formatting | bytes 786432

commit v2 on v0

v2 whole, which is shorter than its diff:
```python
import functools
import math

import jax
import jax.numpy as jnp
from jax import lax
from jax.experimental import pallas as pl
from jax.experimental.pallas import tpu as pltpu
from jax.sharding import PartitionSpec as P

BLK = 128
HD = 128

masked_score = -1e30
SCALE2 = math.log2(math.e) / math.sqrt(HD)
MESH = pl.DeviceIdType.MESH


def routes(slab_count, band_count):
    slab, band = lax.axis_index("tm"), lax.axis_index("band")
    found = []
    if slab_count > 1:
        found.append(({"tm": slab - 1}, None, slab > 0, slab < slab_count - 1, ("adj", 1), slab < slab_count - 1))
    if band_count == 2:
        found.append(({"band": 1 - band}, band == 0, band == 1, None, ("border", 1 - band), band == 0))
    elif band_count > 2:
        found.append(({"band": band - 1}, None, band > 0, band < band_count - 1, ("border", 0), band < band_count - 1))
        found.append(({"band": band + 1}, band < band_count - 1, None, band > 0, ("border", 1), None))
    if slab_count > 1:
        found.append(({"tm": slab + 1}, slab < slab_count - 1, None, slab > 0, ("adj", 0), None))
    return found


def when(condition):
    return (lambda body: body()) if condition is None else pl.when(condition)


def value_chunks(heads):
    return [(0, (heads - 1) * BLK), ((heads - 1) * BLK, BLK)]


def ahead_parts(heads):
    return [(0, BLK)]


def weigh(query, key):
    scores = lax.dot_general(
        query, key, (((1,), (1,)), ((), ())), preferred_element_type=jnp.float32
    )
    return scores * SCALE2


def kernel(
    slab_count, band_count, q_hbm, k_hbm, v_hbm, adj_hbm, border_hbm, out_ref,
    q_ref, k_ref, v_ref, adj_ref, border_ref, send_ref, recv_ref, acc_ref, weights_ref,
    both_ref, peer_adj_ref, peer_border_ref,
    load_sem, here_sem, send_sem, recv_sem, ahead_send_sem, ahead_recv_sem,
):
    plan = routes(slab_count, band_count)
    slots = range(len(plan))
    rows, width = q_ref.shape
    heads = width // HD
    late = lax.axis_index("head") > 0
    early = jnp.logical_not(late)

    neighbours = []
    for axis, count in (("tm", slab_count), ("band", band_count)):
        if count > 1:
            index = lax.axis_index(axis)
            neighbours.append((axis, index, index > 0, index < count - 1))

    barrier = pltpu.get_barrier_semaphore()
    for axis, index, _, has_upper in neighbours:
        @pl.when(has_upper)
        def _():
            pl.semaphore_signal(barrier, inc=1, device_id={axis: index + 1}, device_id_type=MESH)

    loads = [
        pltpu.make_async_copy(source, target, load_sem.at[number])
        for number, (source, target) in enumerate(
            ((k_hbm, k_ref), (adj_hbm, adj_ref), (border_hbm, border_ref), (v_hbm, v_ref), (q_hbm, q_ref))
        )
    ]
    for load in loads[:3]:
        load.start()

    chunks = [[(0, heads * BLK)], value_chunks(heads)]
    pieces_ahead = ahead_parts(heads)
    skipped = sum(size for _, size in pieces_ahead)

    def transfer(slot, part, group, skip=0):
        start, size = chunks[part][group]
        at = (slot, part, pl.ds(start + skip, size - skip))
        return pltpu.make_async_remote_copy(
            src_ref=send_ref.at[at],
            dst_ref=recv_ref.at[at],
            send_sem=send_sem.at[slot, part, group],
            recv_sem=recv_sem.at[slot, part, group],
            device_id=plan[slot][0],
            device_id_type=MESH,
        )

    def ahead(slot):
        mask = (adj_hbm, peer_adj_ref) if plan[slot][4][0] == "adj" else (border_hbm, peer_border_ref)
        parts = [
            (k_hbm.at[:, pl.ds(0, size), pl.ds(head * HD, HD)], both_ref.at[slot, head, :, pl.ds(0, size)])
            for head, size in pieces_ahead
        ]
        return [
            pltpu.make_async_remote_copy(
                src_ref=source,
                dst_ref=target,
                send_sem=ahead_send_sem.at[slot, number],
                recv_sem=ahead_recv_sem.at[slot, number],
                device_id=plan[slot][0],
                device_id_type=MESH,
            )
            for number, (source, target) in enumerate(parts + [mask])
        ]

    def send(slot, part, downward):
        _, up, down, _, _, above = plan[slot]
        sends = down if downward else up
        if sends is None:
            return
        for group in range(len(chunks[part])):
            if downward and part == 0 and above is not None:
                @pl.when(sends & late)
                def _():
                    transfer(slot, part, group, skipped).start()

                @pl.when(sends & early)
                def _():
                    transfer(slot, part, group).start()
            else:
                @pl.when(sends)
                def _():
                    transfer(slot, part, group).start()

    arrivals = sum(lower.astype(jnp.int32) for _, _, lower, _ in neighbours)

    @pl.when(arrivals > 0)
    def _():
        pl.semaphore_wait(barrier, arrivals)

    for slot, (_, _, down, _, _, above) in enumerate(plan):
        if above is not None:
            @pl.when(down & late)
            def _():
                for copy in ahead(slot):
                    copy.start()

    for number, (axis, index, has_lower, _) in enumerate(neighbours):
        @pl.when(has_lower)
        def _():
            pl.semaphore_signal(
                here_sem.at[number], inc=1, device_id={axis: index - 1}, device_id_type=MESH
            )

    for load in loads[3:]:
        load.start()
    for load in loads[1:3]:
        load.wait()
    blocks = [
        adj_ref[row, 1] if kind == "adj" else border_ref[0, row] for _, _, _, _, (kind, row), _ in plan
    ]

    def pick(slot, part, whole):
        for head in range(heads):
            send_ref[slot, part, head * BLK : (head + 1) * BLK] = whole[
                blocks[slot], :, head * HD : (head + 1) * HD
            ]

    loads[0].wait()
    for slot in slots:
        pick(slot, 0, k_ref)
        send(slot, 0, True)
    for number, (_, _, _, has_upper) in enumerate(neighbours):
        @pl.when(has_upper)
        def _():
            pl.semaphore_wait(here_sem.at[number], 1)
    for slot in slots:
        send(slot, 0, False)

    loads[3].wait()
    for slot in slots:
        pick(slot, 1, v_ref)

    def send_values():
        for slot in slots:
            send(slot, 1, True)
            send(slot, 1, False)

    pl.when(early)(send_values)

    for slot, (_, _, _, comes, _, _) in enumerate(plan):
        if comes is not None:
            @pl.when(jnp.logical_not(comes))
            def _():
                recv_ref[slot] = jnp.zeros(recv_ref.shape[1:], recv_ref.dtype)

    loads[4].wait()
    own = []
    for head in range(heads):
        columns = slice(head * HD, (head + 1) * HD)
        scores = weigh(q_ref[:, columns], k_ref[:, :, columns].reshape(rows, HD))
        most = jnp.max(scores, axis=1, keepdims=True)
        weights = jnp.exp2(scores - most)
        total = jnp.sum(weights, axis=1, keepdims=True)
        acc_ref[head] = jnp.dot(
            weights.astype(jnp.bfloat16), v_ref[:, :, columns].reshape(rows, HD), preferred_element_type=jnp.float32
        )
        own.append((most, total))

    for slot, (*_, above) in enumerate(plan):
        if above is not None:
            @pl.when(above & late)
            def _():
                for copy in ahead(slot):
                    copy.wait_recv()

    for slot, (_, _, _, comes, (kind, _), above) in enumerate(plan):
        if above is None:
            @when(comes)
            def _():
                transfer(slot, 0, 0).wait_recv()
        else:
            @pl.when(above & late)
            def _():
                block = peer_adj_ref[1, 1] if kind == "adj" else peer_border_ref[0, 0]
                for head, size in pieces_ahead:
                    recv_ref[slot, 0, head * BLK : head * BLK + size] = both_ref[slot, head, block, :size]
                transfer(slot, 0, 0, skipped).wait_recv()

            whole = jnp.logical_not(above & late)

            @pl.when(whole if comes is None else whole & comes)
            def _():
                transfer(slot, 0, 0).wait_recv()

    pl.when(late)(send_values)

    def arrived(part, head):
        return jnp.concatenate(
            [recv_ref[slot, part, head * BLK : (head + 1) * BLK] for slot in slots], axis=0
        )

    hidden = [
        None if comes is None else jnp.where(comes, 0.0, masked_score).astype(jnp.float32)
        for _, _, _, comes, _, _ in plan
    ]
    for head in range(heads):
        columns = slice(head * HD, (head + 1) * HD)
        scores = weigh(q_ref[:, columns], arrived(0, head))
        scores = [
            scores[:, slot * BLK : (slot + 1) * BLK] + (0.0 if hidden[slot] is None else hidden[slot]) for slot in slots
        ]
        most, total = own[head]
        largest = jnp.maximum(
            most, jnp.max(functools.reduce(jnp.maximum, scores), axis=1, keepdims=True)
        )
        weights = [jnp.exp2(score - largest) for score in scores]
        factor = jnp.exp2(most - largest)
        share = 1.0 / (factor * total + jnp.sum(sum(weights), axis=1, keepdims=True))
        acc_ref[head] = acc_ref[head] * (factor * share)
        for slot in slots:
            weights_ref[head, :, slot * BLK : (slot + 1) * BLK] = (weights[slot] * share).astype(jnp.bfloat16)

    for group, (start, size) in enumerate(chunks[1]):
        for slot, (_, _, _, comes, _, _) in enumerate(plan):
            @when(comes)
            def _():
                transfer(slot, 1, group).wait_recv()
        for head in range(start // BLK, (start + size) // BLK):
            result = acc_ref[head] + jnp.dot(
                weights_ref[head], arrived(1, head), preferred_element_type=jnp.float32
            )
            out_ref[:, head * HD : (head + 1) * HD] = result.astype(out_ref.dtype)

    for slot, (_, up, down, _, _, above) in enumerate(plan):
        sends = down if up is None else up if down is None else None
        if above is None:
            @when(sends)
            def _():
                transfer(slot, 0, 0).wait_send()
        else:
            @pl.when(down & late)
            def _():
                for copy in ahead(slot):
                    copy.wait_send()
                transfer(slot, 0, 0, skipped).wait_send()

            whole = jnp.logical_not(down & late)

            @pl.when(whole if sends is None else whole & sends)
            def _():
                transfer(slot, 0, 0).wait_send()
        for group in range(len(chunks[1])):
            @when(sends)
            def _():
                transfer(slot, 1, group).wait_send()


def per_device(queries, keys, values, adj_mask, border_blocks):
    rows, width = queries.shape[2:]
    heads = width // HD
    slab_count, band_count = lax.axis_size("tm"), lax.axis_size("band")
    sources = (2 if slab_count > 1 else 0) + min(band_count - 1, 2)
    assert rows == 2 * BLK and adj_mask.shape[3] == 2 and border_blocks.shape[3] == 1
    pieces = len(ahead_parts(heads))
    block_sems = pltpu.SemaphoreType.DMA((sources, 2, len(value_chunks(heads))))
    ahead_sems = pltpu.SemaphoreType.DMA((sources, pieces + 1))
    attended = pl.pallas_call(
        functools.partial(kernel, slab_count, band_count),
        out_shape=pltpu.VMEM((rows, width), jnp.bfloat16),
        in_specs=[pl.BlockSpec(memory_space=pl.ANY)] * 5,
        out_specs=pl.BlockSpec(memory_space=pltpu.VMEM),
        scratch_shapes=[
            pltpu.VMEM((rows, width), jnp.bfloat16),
            pltpu.VMEM((rows // BLK, BLK, width), jnp.bfloat16),
            pltpu.VMEM((rows // BLK, BLK, width), jnp.bfloat16),
            pltpu.SMEM(adj_mask.shape[2:], jnp.int32),
            pltpu.SMEM(border_blocks.shape[:1:-1], jnp.int32),
            pltpu.VMEM((sources, 2, heads * BLK, HD), jnp.bfloat16),
            pltpu.VMEM((sources, 2, heads * BLK, HD), jnp.bfloat16),
            pltpu.VMEM((heads, rows, HD), jnp.float32),
            pltpu.VMEM((heads, rows, sources * BLK), jnp.bfloat16),
            pltpu.VMEM((sources, pieces, rows // BLK, BLK, HD), jnp.bfloat16),
            pltpu.SMEM(adj_mask.shape[2:], jnp.int32),
            pltpu.SMEM(border_blocks.shape[:1:-1], jnp.int32),
            pltpu.SemaphoreType.DMA((5,)),
            pltpu.SemaphoreType.REGULAR((max(1, (slab_count > 1) + (band_count > 1)),)),
            block_sems,
            block_sems,
            ahead_sems,
            ahead_sems,
        ],
        compiler_params=pltpu.CompilerParams(collective_id=0, has_side_effects=True),
        name="radial_attention",
    )(
        queries[0, 0],
        keys.reshape(rows // BLK, BLK, width),
        values.reshape(rows // BLK, BLK, width),
        adj_mask[0, 0], border_blocks[0, 0].T,
    )
    return attended[None, None]


def solution(mesh):
    placed = (
        P(("clip", "tm"), "band", None, "head"),
        P(("clip", "tm"), "band", None, "head"),
        P(("clip", "tm"), "band", None, "head"),
        P(("clip", "tm"), "band", None, None),
        P(("clip", "tm"), "band", None, None),
    )
    return jax.shard_map(
        per_device,
        mesh=mesh,
        in_specs=placed,
        out_specs=P(("clip", "tm"), "band", None, "head"),
        check_vma=False,
    )
```

time: 14.8 us -> 13.8 us (0.932)
  the two profiles are of different devices: /device:TPU:0 before, /device:TPU:1 now
where the time goes in v2:
time: 13.8 us; the launch traced here: 13.6 us
  Pallas kernels  12.9 us (93%)
  local copies, waits for them, and re-layouts  0.75 us (5%)
    pallas_call x1, Pallas kernels, per_device(): pl.pallas_call(functools.partial(kernel, slab_count, band_count), out_sha...  12.9 us
    unnamed x1, local copies, waits for them, and re-layouts  0.75 us

profile of v2, /device:TPU:1, one launch (start us, length us, event | category | flops | bytes accessed | tf_op | source)
XLA Modules:
  0.0 13.6 jit_solution(6078686245452398534)
XLA Ops:
  0.0 12.9 %radial_attention.1 = bf16[256,768]{1,0:T(8,128)(2,1)S(1)} custom-call(bf16[256,768]{1,0:T(8,128)(2,1)} %bitcast.7, bf16[2,128,768]{2,1,0:T(8,128)(2,1)} %bitcast.8, bf16[2,128,768]{2,1,0:T(8,128)(2,1)} %bitcast.9, s32[2,2]{1,0:T(2,128)} %bitcast.10, s32[1,2]{1,0:T(1,128)} %bitcast.11), custom_call_target="tpu_custom_call" | custom-call | tf_op jit(solution)/shard_map/radial_attention/pallas_call | solution.py:313
  12.9 0.7 %copy.7 = bf16[1,1,256,768]{3,2,1,0:T(8,128)(2,1)} copy(bf16[1,1,256,768]{3,2,1,0:T(8,128)(2,1)S(1)} %bitcast.6) | data formatting | bytes 786432

commit v3 on v2

--- a/solution.py
+++ b/solution.py
@@ -14,6 +14,9 @@
 masked_score = -1e30
 SCALE2 = math.log2(math.e) / math.sqrt(HD)
 MESH = pl.DeviceIdType.MESH
+
+ROUTE_X = ((0, 0, 1), (1, 0, 1))
+ROUTE_Z = ((0, 1, 0), (1, 1, 0))
 
 
 def routes(slab_count, band_count):
@@ -51,10 +54,11 @@
 
 
 def kernel(
-    slab_count, band_count, q_hbm, k_hbm, v_hbm, adj_hbm, border_hbm, out_ref,
-    q_ref, k_ref, v_ref, adj_ref, border_ref, send_ref, recv_ref, acc_ref, weights_ref,
-    both_ref, peer_adj_ref, peer_border_ref,
-    load_sem, here_sem, send_sem, recv_sem, ahead_send_sem, ahead_recv_sem,
+    clip_count, slab_count, band_count, q_hbm, k_hbm, v_hbm, adj_hbm, border_hbm, out_ref,
+    q_ref, k_ref, v_ref, adj_ref, border_ref, send_ref, recv_ref, acc_ref, weights_ref, share_ref,
+    both_ref, pass_ref, peer_adj_ref, peer_border_ref,
+    load_sem, here_sem, send_sem, recv_sem, ahead_send_sem, ahead_recv_sem, pass_send_sem, pass_recv_sem,
+    relay_send_sem, relay_recv_sem,
 ):
     plan = routes(slab_count, band_count)
     slots = range(len(plan))
@@ -64,10 +68,48 @@
     early = jnp.logical_not(late)
 
     neighbours = []
-    for axis, count in (("tm", slab_count), ("band", band_count)):
+    for axis, count in (("tm", slab_count), ("band", band_count), ("clip", clip_count)):
         if count > 1:
             index = lax.axis_index(axis)
-            neighbours.append((axis, index, index > 0, index < count - 1))
+            lower, upper = index > 0, index < count - 1
+            if axis == "clip":
+                lower, upper = lower & late, upper & late
+            neighbours.append((axis, index, lower, upper))
+    others = sum(axis != "clip" for axis, *_ in neighbours)
+
+    detours = {}
+    if clip_count > 1 and slab_count > 1 and band_count > 1:
+        for slot, (_, _, _, _, (kind, _), above) in enumerate(plan):
+            if above is not None:
+                detours[slot] = ROUTE_X if kind == "border" else ROUTE_Z
+
+    def at(clip, slab, band):
+        place = [lax.axis_index(axis) for axis in ("clip", "tm", "band")]
+        return (place[0] == clip) & (place[1] == slab) & (place[2] == band) & late
+
+    lends = {slot: at(*source) for slot, (source, _) in detours.items()}
+    relays = {slot: at(*middle) for slot, (_, middle) in detours.items()}
+    corner = at(0, 0, 0)
+
+    def lend(slot):
+        return pltpu.make_async_remote_copy(
+            src_ref=send_ref.at[slot, 1, pl.ds(0, BLK)],
+            dst_ref=pass_ref.at[slot],
+            send_sem=pass_send_sem.at[slot],
+            recv_sem=pass_recv_sem.at[slot],
+            device_id=dict(zip(("clip", "tm", "band"), detours[slot][1])),
+            device_id_type=MESH,
+        )
+
+    def relay(slot):
+        return pltpu.make_async_remote_copy(
+            src_ref=pass_ref.at[slot],
+            dst_ref=recv_ref.at[slot, 1, pl.ds(0, BLK)],
+            send_sem=relay_send_sem.at[slot],
+            recv_sem=relay_recv_sem.at[slot],
+            device_id={"clip": 0, "tm": 0, "band": 0},
+            device_id_type=MESH,
+        )
 
     barrier = pltpu.get_barrier_semaphore()
     for axis, index, _, has_upper in neighbours:
@@ -124,12 +166,15 @@
         if sends is None:
             return
         for group in range(len(chunks[part])):
-            if downward and part == 0 and above is not None:
-                @pl.when(sends & late)
-                def _():
-                    transfer(slot, part, group, skipped).start()
-
-                @pl.when(sends & early)
+            short, skip = late, skipped
+            if part:
+                short, skip = lends.get(slot), BLK
+            if downward and group == 0 and above is not None and short is not None:
+                @pl.when(sends & short)
+                def _():
+                    transfer(slot, part, group, skip).start()
+
+                @pl.when(sends & jnp.logical_not(short))
                 def _():
                     transfer(slot, part, group).start()
             else:
@@ -175,7 +220,7 @@
     for slot in slots:
         pick(slot, 0, k_ref)
         send(slot, 0, True)
-    for number, (_, _, _, has_upper) in enumerate(neighbours):
+    for number, (_, _, _, has_upper) in enumerate(neighbours[:others]):
         @pl.when(has_upper)
         def _():
             pl.semaphore_wait(here_sem.at[number], 1)
@@ -185,6 +230,14 @@
     loads[3].wait()
     for slot in slots:
         pick(slot, 1, v_ref)
+    if clip_count > 1:
+        @pl.when(neighbours[others][3])
+        def _():
+            pl.semaphore_wait(here_sem.at[others], 1)
+    for slot in detours:
+        @pl.when(lends[slot])
+        def _():
+            lend(slot).start()
 
     def send_values():
         for slot in slots:
@@ -237,6 +290,12 @@
             @pl.when(whole if comes is None else whole & comes)
             def _():
                 transfer(slot, 0, 0).wait_recv()
+
+    for slot in detours:
+        @pl.when(relays[slot])
+        def _():
+            lend(slot).wait_recv()
+            relay(slot).start()
 
     pl.when(late)(send_values)
 
@@ -262,20 +321,33 @@
         weights = [jnp.exp2(score - largest) for score in scores]
         factor = jnp.exp2(most - largest)
         share = 1.0 / (factor * total + jnp.sum(sum(weights), axis=1, keepdims=True))
-        acc_ref[head] = acc_ref[head] * (factor * share)
+        acc_ref[head] = acc_ref[head] * factor
+        share_ref[head] = jnp.broadcast_to(share, (rows, HD))
         for slot in slots:
-            weights_ref[head, :, slot * BLK : (slot + 1) * BLK] = (weights[slot] * share).astype(jnp.bfloat16)
+            weights_ref[head, :, slot * BLK : (slot + 1) * BLK] = weights[slot].astype(jnp.bfloat16)
 
     for group, (start, size) in enumerate(chunks[1]):
         for slot, (_, _, _, comes, _, _) in enumerate(plan):
-            @when(comes)
-            def _():
-                transfer(slot, 1, group).wait_recv()
+            if slot in detours and group == 0:
+                @pl.when(corner)
+                def _():
+                    relay(slot).wait_recv()
+                    transfer(slot, 1, group, BLK).wait_recv()
+
+                whole = jnp.logical_not(corner)
+
+                @pl.when(whole if comes is None else whole & comes)
+                def _():
+                    transfer(slot, 1, group).wait_recv()
+            else:
+                @when(comes)
+                def _():
+                    transfer(slot, 1, group).wait_recv()
         for head in range(start // BLK, (start + size) // BLK):
             result = acc_ref[head] + jnp.dot(
                 weights_ref[head], arrived(1, head), preferred_element_type=jnp.float32
             )
-            out_ref[:, head * HD : (head + 1) * HD] = result.astype(out_ref.dtype)
+            out_ref[:, head * HD : (head + 1) * HD] = (result * share_ref[head]).astype(out_ref.dtype)
 
     for slot, (_, up, down, _, _, above) in enumerate(plan):
         sends = down if up is None else up if down is None else None
@@ -296,22 +368,38 @@
             def _():
                 transfer(slot, 0, 0).wait_send()
         for group in range(len(chunks[1])):
-            @when(sends)
-            def _():
-                transfer(slot, 1, group).wait_send()
+            if slot in detours and group == 0:
+                @pl.when(lends[slot])
+                def _():
+                    lend(slot).wait_send()
+                    transfer(slot, 1, group, BLK).wait_send()
+
+                @pl.when(relays[slot])
+                def _():
+                    relay(slot).wait_send()
+
+                whole = jnp.logical_not(lends[slot])
+
+                @pl.when(whole if sends is None else whole & sends)
+                def _():
+                    transfer(slot, 1, group).wait_send()
+            else:
+                @when(sends)
+                def _():
+                    transfer(slot, 1, group).wait_send()
 
 
 def per_device(queries, keys, values, adj_mask, border_blocks):
     rows, width = queries.shape[2:]
     heads = width // HD
-    slab_count, band_count = lax.axis_size("tm"), lax.axis_size("band")
+    clip_count, slab_count, band_count = (lax.axis_size(axis) for axis in ("clip", "tm", "band"))
     sources = (2 if slab_count > 1 else 0) + min(band_count - 1, 2)
     assert rows == 2 * BLK and adj_mask.shape[3] == 2 and border_blocks.shape[3] == 1
     pieces = len(ahead_parts(heads))
     block_sems = pltpu.SemaphoreType.DMA((sources, 2, len(value_chunks(heads))))
     ahead_sems = pltpu.SemaphoreType.DMA((sources, pieces + 1))
     attended = pl.pallas_call(
-        functools.partial(kernel, slab_count, band_count),
+        functools.partial(kernel, clip_count, slab_count, band_count),
         out_shape=pltpu.VMEM((rows, width), jnp.bfloat16),
         in_specs=[pl.BlockSpec(memory_space=pl.ANY)] * 5,
         out_specs=pl.BlockSpec(memory_space=pltpu.VMEM),
@@ -325,15 +413,21 @@
             pltpu.VMEM((sources, 2, heads * BLK, HD), jnp.bfloat16),
             pltpu.VMEM((heads, rows, HD), jnp.float32),
             pltpu.VMEM((heads, rows, sources * BLK), jnp.bfloat16),
+            pltpu.VMEM((heads, rows, HD), jnp.float32),
             pltpu.VMEM((sources, pieces, rows // BLK, BLK, HD), jnp.bfloat16),
+            pltpu.VMEM((sources, BLK, HD), jnp.bfloat16),
             pltpu.SMEM(adj_mask.shape[2:], jnp.int32),
             pltpu.SMEM(border_blocks.shape[:1:-1], jnp.int32),
             pltpu.SemaphoreType.DMA((5,)),
-            pltpu.SemaphoreType.REGULAR((max(1, (slab_count > 1) + (band_count > 1)),)),
+            pltpu.SemaphoreType.REGULAR((max(1, (slab_count > 1) + (band_count > 1) + (clip_count > 1)),)),
             block_sems,
             block_sems,
             ahead_sems,
             ahead_sems,
+            pltpu.SemaphoreType.DMA((sources,)),
+            pltpu.SemaphoreType.DMA((sources,)),
+            pltpu.SemaphoreType.DMA((sources,)),
+            pltpu.SemaphoreType.DMA((sources,)),
         ],
         compiler_params=pltpu.CompilerParams(collective_id=0, has_side_effects=True),
         name="radial_attention",

time: 13.8 us -> 13.5 us (0.978)
  Pallas kernels: 12.9 us -> 12.6 us
    pallas_call x1, Pallas kernels: 12.9 us -> 12.6 us  [per_device(): pl.pallas_call(functools.partial(kernel, clip_count, slab_count, band_cou...]
where the time goes in v3:
time: 13.5 us; the launch traced here: 13.4 us
  Pallas kernels  12.6 us (93%)
  local copies, waits for them, and re-layouts  0.75 us (6%)
    pallas_call x1, Pallas kernels, per_device(): pl.pallas_call(functools.partial(kernel, clip_count, slab_count, band_cou...  12.6 us
    unnamed x1, local copies, waits for them, and re-layouts  0.75 us

profile of v3, /device:TPU:1, one launch (start us, length us, event | category | flops | bytes accessed | tf_op | source)
XLA Modules:
  0.0 13.4 jit_solution(17361283786997890267)
XLA Ops:
  0.0 12.6 %radial_attention.1 = bf16[256,768]{1,0:T(8,128)(2,1)S(1)} custom-call(bf16[256,768]{1,0:T(8,128)(2,1)} %bitcast.7, bf16[2,128,768]{2,1,0:T(8,128)(2,1)} %bitcast.8, bf16[2,128,768]{2,1,0:T(8,128)(2,1)} %bitcast.9, s32[2,2]{1,0:T(2,128)} %bitcast.10, s32[1,2]{1,0:T(1,128)} %bitcast.11), custom_call_target="tpu_custom_call" | custom-call | tf_op jit(solution)/shard_map/radial_attention/pallas_call | solution.py:401
  12.6 0.7 %copy.7 = bf16[1,1,256,768]{3,2,1,0:T(8,128)(2,1)} copy(bf16[1,1,256,768]{3,2,1,0:T(8,128)(2,1)S(1)} %bitcast.6) | data formatting | bytes 786432

commit v4 on v3

--- a/solution.py
+++ b/solution.py
@@ -14,6 +14,7 @@
 masked_score = -1e30
 SCALE2 = math.log2(math.e) / math.sqrt(HD)
 MESH = pl.DeviceIdType.MESH
+TAIL = 1
 
 ROUTE_X = ((0, 0, 1), (1, 0, 1))
 ROUTE_Z = ((0, 1, 0), (1, 1, 0))
@@ -38,8 +39,13 @@
     return (lambda body: body()) if condition is None else pl.when(condition)
 
 
+def last_heads(heads):
+    return TAIL if heads > 2 * TAIL else 1
+
+
 def value_chunks(heads):
-    return [(0, (heads - 1) * BLK), ((heads - 1) * BLK, BLK)]
+    most = heads - last_heads(heads)
+    return [(0, most * BLK), (most * BLK, (heads - most) * BLK)]
 
 
 def ahead_parts(heads):
@@ -54,7 +60,8 @@
 
 
 def kernel(
-    clip_count, slab_count, band_count, q_hbm, k_hbm, v_hbm, adj_hbm, border_hbm, out_ref,
+    clip_count, slab_count, band_count, q_hbm, k_hbm, v_hbm, adj_hbm, border_hbm,
+    out_ref, last_acc_ref, last_weights_ref, last_share_ref, last_recv_ref,
     q_ref, k_ref, v_ref, adj_ref, border_ref, send_ref, recv_ref, acc_ref, weights_ref, share_ref,
     both_ref, pass_ref, peer_adj_ref, peer_border_ref,
     load_sem, here_sem, send_sem, recv_sem, ahead_send_sem, ahead_recv_sem, pass_send_sem, pass_recv_sem,
@@ -135,7 +142,7 @@
         at = (slot, part, pl.ds(start + skip, size - skip))
         return pltpu.make_async_remote_copy(
             src_ref=send_ref.at[at],
-            dst_ref=recv_ref.at[at],
+            dst_ref=last_recv_ref.at[slot] if group else recv_ref.at[at],
             send_sem=send_sem.at[slot, part, group],
             recv_sem=recv_sem.at[slot, part, group],
             device_id=plan[slot][0],
@@ -251,6 +258,15 @@
             @pl.when(jnp.logical_not(comes))
             def _():
                 recv_ref[slot] = jnp.zeros(recv_ref.shape[1:], recv_ref.dtype)
+                last_recv_ref[slot] = jnp.zeros(last_recv_ref.shape[1:], recv_ref.dtype)
+
+    first_last = heads - last_acc_ref.shape[0]
+
+    def kept(head):
+        if head < first_last:
+            return acc_ref.at[head], weights_ref.at[head], share_ref.at[head]
+        number = head - first_last
+        return last_acc_ref.at[number], last_weights_ref.at[number], last_share_ref.at[number]
 
     loads[4].wait()
     own = []
@@ -260,7 +276,7 @@
         most = jnp.max(scores, axis=1, keepdims=True)
         weights = jnp.exp2(scores - most)
         total = jnp.sum(weights, axis=1, keepdims=True)
-        acc_ref[head] = jnp.dot(
+        kept(head)[0][...] = jnp.dot(
             weights.astype(jnp.bfloat16), v_ref[:, :, columns].reshape(rows, HD), preferred_element_type=jnp.float32
         )
         own.append((most, total))
@@ -321,10 +337,11 @@
         weights = [jnp.exp2(score - largest) for score in scores]
         factor = jnp.exp2(most - largest)
         share = 1.0 / (factor * total + jnp.sum(sum(weights), axis=1, keepdims=True))
-        acc_ref[head] = acc_ref[head] * factor
-        share_ref[head] = jnp.broadcast_to(share, (rows, HD))
+        sum_ref, part_ref, scale_ref = kept(head)
+        sum_ref[...] = sum_ref[...] * factor
+        scale_ref[...] = jnp.broadcast_to(share, (rows, HD))
         for slot in slots:
-            weights_ref[head, :, slot * BLK : (slot + 1) * BLK] = weights[slot].astype(jnp.bfloat16)
+            part_ref[:, slot * BLK : (slot + 1) * BLK] = weights[slot].astype(jnp.bfloat16)
 
     for group, (start, size) in enumerate(chunks[1]):
         for slot, (_, _, _, comes, _, _) in enumerate(plan):
@@ -343,7 +360,7 @@
                 @when(comes)
                 def _():
                     transfer(slot, 1, group).wait_recv()
-        for head in range(start // BLK, (start + size) // BLK):
+        for head in range(start // BLK, min((start + size) // BLK, first_last)):
             result = acc_ref[head] + jnp.dot(
                 weights_ref[head], arrived(1, head), preferred_element_type=jnp.float32
             )
@@ -387,6 +404,24 @@
                 @when(sends)
                 def _():
                     transfer(slot, 1, group).wait_send()
+
+
+def finish(done_ref, acc_ref, weights_ref, share_ref, recv_ref, out_hbm, last_ref, sem):
+    width = done_ref.shape[1]
+    copies = [
+        pltpu.make_async_copy(done_ref, out_hbm.at[:, pl.ds(0, width)], sem.at[0]),
+        pltpu.make_async_copy(last_ref, out_hbm.at[:, pl.ds(width, last_ref.shape[1])], sem.at[1]),
+    ]
+    copies[0].start()
+    for head in range(acc_ref.shape[0]):
+        values = jnp.concatenate(
+            [recv_ref[slot, head * BLK : (head + 1) * BLK] for slot in range(recv_ref.shape[0])], axis=0
+        )
+        result = acc_ref[head] + jnp.dot(weights_ref[head], values, preferred_element_type=jnp.float32)
+        last_ref[:, head * HD : (head + 1) * HD] = (result * share_ref[head]).astype(last_ref.dtype)
+    copies[1].start()
+    for copy in copies:
+        copy.wait()
 
 
 def per_device(queries, keys, values, adj_mask, border_blocks):
@@ -398,11 +433,18 @@
     pieces = len(ahead_parts(heads))
     block_sems = pltpu.SemaphoreType.DMA((sources, 2, len(value_chunks(heads))))
     ahead_sems = pltpu.SemaphoreType.DMA((sources, pieces + 1))
-    attended = pl.pallas_call(
+    last = last_heads(heads)
+    parts = pl.pallas_call(
         functools.partial(kernel, clip_count, slab_count, band_count),
-        out_shape=pltpu.VMEM((rows, width), jnp.bfloat16),
+        out_shape=[
+            pltpu.VMEM((rows, width - last * HD), jnp.bfloat16),
+            pltpu.VMEM((last, rows, HD), jnp.float32),
+            pltpu.VMEM((last, rows, sources * BLK), jnp.bfloat16),
+            pltpu.VMEM((last, rows, HD), jnp.float32),
+            pltpu.VMEM((sources, last * BLK, HD), jnp.bfloat16),
+        ],
         in_specs=[pl.BlockSpec(memory_space=pl.ANY)] * 5,
-        out_specs=pl.BlockSpec(memory_space=pltpu.VMEM),
+        out_specs=[pl.BlockSpec(memory_space=pltpu.VMEM)] * 5,
         scratch_shapes=[
             pltpu.VMEM((rows, width), jnp.bfloat16),
             pltpu.VMEM((rows // BLK, BLK, width), jnp.bfloat16),
@@ -437,6 +479,14 @@
         values.reshape(rows // BLK, BLK, width),
         adj_mask[0, 0], border_blocks[0, 0].T,
     )
+    attended = pl.pallas_call(
+        finish,
+        out_shape=jax.ShapeDtypeStruct((rows, width), jnp.bfloat16),
+        in_specs=[pl.BlockSpec(memory_space=pltpu.VMEM)] * 5,
+        out_specs=pl.BlockSpec(memory_space=pl.ANY),
+        scratch_shapes=[pltpu.VMEM((rows, last * HD), jnp.bfloat16), pltpu.SemaphoreType.DMA((2,))],
+        name="last_heads",
+    )(*(pltpu.with_memory_space_constraint(part, pltpu.VMEM) for part in parts))
     return attended[None, None]
 
 

time: 13.5 us -> 13.4 us (level)
  local copies, waits for them, and re-layouts: 0.75 us -> 0 us
  Pallas kernels: 12.6 us -> 13.3 us
    pallas_call x0 -> x1, Pallas kernels: none -> 0.85 us  [per_device(): pl.pallas_call(finish, out_shape=jax.ShapeDtypeStruct((rows, width), jnp....]
    unnamed x1 -> x0, local copies, waits for them, and re-layouts: 0.75 us -> none
    pallas_call x1, Pallas kernels: 12.6 us -> 12.4 us  [per_device(): pl.pallas_call(functools.partial(kernel, clip_count, slab_count, band_cou...]
where the time goes in v4:
time: 13.4 us; the launch traced here: 13.3 us
  Pallas kernels  13.3 us (99%)
    pallas_call x1, Pallas kernels, per_device(): pl.pallas_call(functools.partial(kernel, clip_count, slab_count, band_cou...  12.4 us
    pallas_call x1, Pallas kernels, per_device(): pl.pallas_call(finish, out_shape=jax.ShapeDtypeStruct((rows, width), jnp....  0.85 us

profile of v4, /device:TPU:1, one launch (start us, length us, event | category | flops | bytes accessed | tf_op | source)
XLA Modules:
  0.0 13.3 jit_solution(2129594720732789906)
XLA Ops:
  0.0 12.4 %radial_attention.1 = (bf16[256,640]{1,0:T(8,128)(2,1)S(1)}, f32[1,256,128]{2,1,0:T(8,128)S(1)}, bf16[1,256,384]{2,1,0:T(8,128)(2,1)S(1)}, f32[1,256,128]{2,1,0:T(8,128)S(1)}, bf16[3,128,128]{2,1,0:T(8,128)(2,1)S(1)}) custom-call(bf16[256,768]{1,0:T(8,128)(2,1)} %bitcast.6, bf16[2,128,768]{2,1,0:T(8,128)(2,1)} %bitcast.7, bf16[2,128,768]{2,1,0:T(8,128)(2,1)} %bitcast.8, ...), custom_call_target="tpu_custom_call" | custom-call | tf_op jit(solution)/shard_map/radial_attention/pallas_call | solution.py:437
  12.4 0.8 %last_heads.1 = bf16[256,768]{1,0:T(8,128)(2,1)} custom-call(bf16[256,640]{1,0:T(8,128)(2,1)S(1)} %get-tuple-element.10.done_ref, f32[1,256,128]{2,1,0:T(8,128)S(1)} %get-tuple-element.11.acc_ref, bf16[1,256,384]{2,1,0:T(8,128)(2,1)S(1)} %get-tuple-element.12.weights_ref, f32[1,256,128]{2,1,0:T(8,128)S(1)} %get-tuple-element.13.share_ref, ...), custom_call_target="tpu_custom_call" | custom-call | tf_op jit(solution)/shard_map/last_heads/pallas_call | solution.py:482

commit v5 on v4

--- a/solution.py
+++ b/solution.py
@@ -48,8 +48,7 @@
     return [(0, most * BLK), (most * BLK, (heads - most) * BLK)]
 
 
-def ahead_parts(heads):
-    return [(0, BLK)]
+FLAG = 16
 
 
 def weigh(query, key):
@@ -62,14 +61,13 @@
 def kernel(
     clip_count, slab_count, band_count, q_hbm, k_hbm, v_hbm, adj_hbm, border_hbm,
     out_ref, last_acc_ref, last_weights_ref, last_share_ref, last_recv_ref,
-    q_ref, k_ref, v_ref, adj_ref, border_ref, send_ref, recv_ref, acc_ref, weights_ref, share_ref,
-    both_ref, pass_ref, peer_adj_ref, peer_border_ref,
-    load_sem, here_sem, send_sem, recv_sem, ahead_send_sem, ahead_recv_sem, pass_send_sem, pass_recv_sem,
-    relay_send_sem, relay_recv_sem,
+    vq_ref, k_ref, adj_ref, border_ref, send_ref, recv_ref, acc_ref, weights_ref, share_ref,
+    both_ref, pass_ref,
+    load_sem, here_sem, send_sem, ahead_sem, pass_sem, key_sem, value_sem,
 ):
     plan = routes(slab_count, band_count)
     slots = range(len(plan))
-    rows, width = q_ref.shape
+    rows, width = k_ref.shape[0] * BLK, k_ref.shape[2]
     heads = width // HD
     late = lax.axis_index("head") > 0
     early = jnp.logical_not(late)
@@ -82,7 +80,6 @@
             if axis == "clip":
                 lower, upper = lower & late, upper & late
             neighbours.append((axis, index, lower, upper))
-    others = sum(axis != "clip" for axis, *_ in neighbours)
 
     detours = {}
     if clip_count > 1 and slab_count > 1 and band_count > 1:
@@ -96,14 +93,16 @@
 
     lends = {slot: at(*source) for slot, (source, _) in detours.items()}
     relays = {slot: at(*middle) for slot, (_, middle) in detours.items()}
-    corner = at(0, 0, 0)
+
+    def base(slot, part):
+        return (slot * 2 + part) * heads * BLK
 
     def lend(slot):
         return pltpu.make_async_remote_copy(
-            src_ref=send_ref.at[slot, 1, pl.ds(0, BLK)],
+            src_ref=send_ref.at[pl.ds(base(slot, 1), BLK)],
             dst_ref=pass_ref.at[slot],
-            send_sem=pass_send_sem.at[slot],
-            recv_sem=pass_recv_sem.at[slot],
+            send_sem=send_sem.at[slot],
+            recv_sem=pass_sem,
             device_id=dict(zip(("clip", "tm", "band"), detours[slot][1])),
             device_id_type=MESH,
         )
@@ -112,8 +111,8 @@
         return pltpu.make_async_remote_copy(
             src_ref=pass_ref.at[slot],
             dst_ref=recv_ref.at[slot, 1, pl.ds(0, BLK)],
-            send_sem=relay_send_sem.at[slot],
-            recv_sem=relay_recv_sem.at[slot],
+            send_sem=send_sem.at[slot],
+            recv_sem=value_sem.at[0],
             device_id={"clip": 0, "tm": 0, "band": 0},
             device_id_type=MESH,
         )
@@ -125,47 +124,52 @@
             pl.semaphore_signal(barrier, inc=1, device_id={axis: index + 1}, device_id_type=MESH)
 
     loads = [
-        pltpu.make_async_copy(source, target, load_sem.at[number])
+        pltpu.make_async_copy(source, target, load_sem.at[min(number, 3)])
         for number, (source, target) in enumerate(
-            ((k_hbm, k_ref), (adj_hbm, adj_ref), (border_hbm, border_ref), (v_hbm, v_ref), (q_hbm, q_ref))
+            (
+                (k_hbm, k_ref), (adj_hbm, adj_ref), (border_hbm, border_ref),
+                (v_hbm, vq_ref.at[pl.ds(0, rows // BLK)]), (q_hbm, vq_ref.at[pl.ds(rows // BLK, rows // BLK)]),
+            )
         )
     ]
     for load in loads[:3]:
         load.start()
 
     chunks = [[(0, heads * BLK)], value_chunks(heads)]
-    pieces_ahead = ahead_parts(heads)
-    skipped = sum(size for _, size in pieces_ahead)
+    skipped = BLK - FLAG
 
     def transfer(slot, part, group, skip=0):
         start, size = chunks[part][group]
-        at = (slot, part, pl.ds(start + skip, size - skip))
+        at = pl.ds(start + skip, size - skip)
         return pltpu.make_async_remote_copy(
-            src_ref=send_ref.at[at],
-            dst_ref=last_recv_ref.at[slot] if group else recv_ref.at[at],
-            send_sem=send_sem.at[slot, part, group],
-            recv_sem=recv_sem.at[slot, part, group],
+            src_ref=send_ref.at[pl.ds(base(slot, part) + start + skip, size - skip)],
+            dst_ref=last_recv_ref.at[slot] if group else recv_ref.at[slot, part, at],
+            send_sem=send_sem.at[slot],
+            recv_sem=value_sem.at[group] if part else key_sem.at[slot],
             device_id=plan[slot][0],
             device_id_type=MESH,
         )
 
     def ahead(slot):
-        mask = (adj_hbm, peer_adj_ref) if plan[slot][4][0] == "adj" else (border_hbm, peer_border_ref)
-        parts = [
-            (k_hbm.at[:, pl.ds(0, size), pl.ds(head * HD, HD)], both_ref.at[slot, head, :, pl.ds(0, size)])
-            for head, size in pieces_ahead
-        ]
-        return [
-            pltpu.make_async_remote_copy(
-                src_ref=source,
-                dst_ref=target,
-                send_sem=ahead_send_sem.at[slot, number],
-                recv_sem=ahead_recv_sem.at[slot, number],
-                device_id=plan[slot][0],
-                device_id_type=MESH,
-            )
-            for number, (source, target) in enumerate(parts + [mask])
-        ]
+        return pltpu.make_async_remote_copy(
+            src_ref=k_hbm.at[:, :, pl.ds(0, HD)],
+            dst_ref=both_ref.at[slot],
+            send_sem=send_sem.at[slot],
+            recv_sem=ahead_sem,
+            device_id=plan[slot][0],
+            device_id_type=MESH,
+        )
+
+    def wait(sem, size):
+        some = send_ref.at[pl.ds(0, size)]
+        pltpu.make_async_copy(some, some, sem).wait()
+
+    def wait_for(conditions, sem, size):
+        count = sum(jnp.int32(1) if condition is None else condition.astype(jnp.int32) for condition in conditions)
+        for number in range(1, len(conditions) + 1):
+            @pl.when(count == number)
+            def _():
+                wait(sem, number * size)
 
     def send(slot, part, downward):
         _, up, down, _, _, above = plan[slot]
@@ -199,48 +203,57 @@
         if above is not None:
             @pl.when(down & late)
             def _():
-                for copy in ahead(slot):
-                    copy.start()
-
-    for number, (axis, index, has_lower, _) in enumerate(neighbours):
+                ahead(slot).start()
+
+    for axis, index, has_lower, _ in neighbours:
         @pl.when(has_lower)
         def _():
-            pl.semaphore_signal(
-                here_sem.at[number], inc=1, device_id={axis: index - 1}, device_id_type=MESH
-            )
+            pl.semaphore_signal(here_sem, inc=1, device_id={axis: index - 1}, device_id_type=MESH)
 
     for load in loads[3:]:
         load.start()
-    for load in loads[1:3]:
+    for load in loads[:3]:
         load.wait()
     blocks = [
         adj_ref[row, 1] if kind == "adj" else border_ref[0, row] for _, _, _, _, (kind, row), _ in plan
     ]
 
-    def pick(slot, part, whole):
-        for head in range(heads):
-            send_ref[slot, part, head * BLK : (head + 1) * BLK] = whole[
-                blocks[slot], :, head * HD : (head + 1) * HD
-            ]
-
-    loads[0].wait()
+    def pick(slot, part, whole, start=0):
+        for head in range(start, heads):
+            to = base(slot, part) + head * BLK
+            send_ref[to : to + BLK] = whole[blocks[slot], :, head * HD : (head + 1) * HD]
+
+    def pick_keys(slot):
+        _, _, down, _, _, above = plan[slot]
+        if above is None:
+            pick(slot, 0, k_ref)
+            return
+        pick(slot, 0, k_ref, 1)
+        to = base(slot, 0)
+
+        @pl.when(down & late)
+        def _():
+            send_ref[to + skipped : to + BLK] = jnp.full((FLAG, HD), blocks[slot].astype(jnp.float32)).astype(jnp.bfloat16)
+
+        @pl.when(jnp.logical_not(down & late))
+        def _():
+            send_ref[to : to + BLK] = k_ref[blocks[slot], :, :HD]
+
     for slot in slots:
-        pick(slot, 0, k_ref)
+        pick_keys(slot)
         send(slot, 0, True)
-    for number, (_, _, _, has_upper) in enumerate(neighbours[:others]):
-        @pl.when(has_upper)
-        def _():
-            pl.semaphore_wait(here_sem.at[number], 1)
+    uppers = sum(upper.astype(jnp.int32) for *_, upper in neighbours)
+
+    @pl.when(uppers > 0)
+    def _():
+        pl.semaphore_wait(here_sem, uppers)
+
     for slot in slots:
         send(slot, 0, False)
 
-    loads[3].wait()
+    pltpu.make_async_copy(vq_ref, vq_ref, load_sem.at[3]).wait()
     for slot in slots:
-        pick(slot, 1, v_ref)
-    if clip_count > 1:
-        @pl.when(neighbours[others][3])
-        def _():
-            pl.semaphore_wait(here_sem.at[others], 1)
+        pick(slot, 1, vq_ref)
     for slot in detours:
         @pl.when(lends[slot])
         def _():
@@ -268,27 +281,23 @@
         number = head - first_last
         return last_acc_ref.at[number], last_weights_ref.at[number], last_share_ref.at[number]
 
-    loads[4].wait()
+    def query(columns):
+        return vq_ref[rows // BLK :, :, columns].reshape(rows, HD)
+
     own = []
     for head in range(heads):
         columns = slice(head * HD, (head + 1) * HD)
-        scores = weigh(q_ref[:, columns], k_ref[:, :, columns].reshape(rows, HD))
+        scores = weigh(query(columns), k_ref[:, :, columns].reshape(rows, HD))
         most = jnp.max(scores, axis=1, keepdims=True)
         weights = jnp.exp2(scores - most)
         total = jnp.sum(weights, axis=1, keepdims=True)
         kept(head)[0][...] = jnp.dot(
-            weights.astype(jnp.bfloat16), v_ref[:, :, columns].reshape(rows, HD), preferred_element_type=jnp.float32
+            weights.astype(jnp.bfloat16), vq_ref[: rows // BLK, :, columns].reshape(rows, HD), preferred_element_type=jnp.float32
         )
         own.append((most, total))
 
-    for slot, (*_, above) in enumerate(plan):
-        if above is not None:
-            @pl.when(above & late)
-            def _():
-                for copy in ahead(slot):
-                    copy.wait_recv()
-
-    for slot, (_, _, _, comes, (kind, _), above) in enumerate(plan):
+    wait_for([above & late for *_, above in plan if above is not None], ahead_sem, rows)
+    for slot, (_, _, _, comes, _, above) in enumerate(plan):
         if above is None:
             @when(comes)
             def _():
@@ -296,10 +305,13 @@
         else:
             @pl.when(above & late)
             def _():
-                block = peer_adj_ref[1, 1] if kind == "adj" else peer_border_ref[0, 0]
-                for head, size in pieces_ahead:
-                    recv_ref[slot, 0, head * BLK : head * BLK + size] = both_ref[slot, head, block, :size]
                 transfer(slot, 0, 0, skipped).wait_recv()
+                flag = recv_ref[slot, 0, skipped:BLK].astype(jnp.float32)
+                recv_ref[slot, 0, :BLK] = jnp.where(
+                    jnp.concatenate([flag] * (BLK // FLAG), axis=0) > 0.5,
+                    both_ref[slot, 1].astype(jnp.float32),
+                    both_ref[slot, 0].astype(jnp.float32),
+                ).astype(jnp.bfloat16)
 
             whole = jnp.logical_not(above & late)
 
@@ -326,7 +338,7 @@
     ]
     for head in range(heads):
         columns = slice(head * HD, (head + 1) * HD)
-        scores = weigh(q_ref[:, columns], arrived(0, head))
+        scores = weigh(query(columns), arrived(0, head))
         scores = [
             scores[:, slot * BLK : (slot + 1) * BLK] + (0.0 if hidden[slot] is None else hidden[slot]) for slot in slots
         ]
@@ -344,22 +356,7 @@
             part_ref[:, slot * BLK : (slot + 1) * BLK] = weights[slot].astype(jnp.bfloat16)
 
     for group, (start, size) in enumerate(chunks[1]):
-        for slot, (_, _, _, comes, _, _) in enumerate(plan):
-            if slot in detours and group == 0:
-                @pl.when(corner)
-                def _():
-                    relay(slot).wait_recv()
-                    transfer(slot, 1, group, BLK).wait_recv()
-
-                whole = jnp.logical_not(corner)
-
-                @pl.when(whole if comes is None else whole & comes)
-                def _():
-                    transfer(slot, 1, group).wait_recv()
-            else:
-                @when(comes)
-                def _():
-                    transfer(slot, 1, group).wait_recv()
+        wait_for([comes for _, _, _, comes, _, _ in plan], value_sem.at[group], size)
         for head in range(start // BLK, min((start + size) // BLK, first_last)):
             result = acc_ref[head] + jnp.dot(
                 weights_ref[head], arrived(1, head), preferred_element_type=jnp.float32
@@ -368,42 +365,29 @@
 
     for slot, (_, up, down, _, _, above) in enumerate(plan):
         sends = down if up is None else up if down is None else None
+        whole = 2 * heads * BLK
         if above is None:
             @when(sends)
             def _():
-                transfer(slot, 0, 0).wait_send()
-        else:
-            @pl.when(down & late)
-            def _():
-                for copy in ahead(slot):
-                    copy.wait_send()
-                transfer(slot, 0, 0, skipped).wait_send()
-
-            whole = jnp.logical_not(down & late)
-
-            @pl.when(whole if sends is None else whole & sends)
-            def _():
-                transfer(slot, 0, 0).wait_send()
-        for group in range(len(chunks[1])):
-            if slot in detours and group == 0:
-                @pl.when(lends[slot])
-                def _():
-                    lend(slot).wait_send()
-                    transfer(slot, 1, group, BLK).wait_send()
-
-                @pl.when(relays[slot])
-                def _():
-                    relay(slot).wait_send()
-
-                whole = jnp.logical_not(lends[slot])
-
-                @pl.when(whole if sends is None else whole & sends)
-                def _():
-                    transfer(slot, 1, group).wait_send()
-            else:
-                @when(sends)
-                def _():
-                    transfer(slot, 1, group).wait_send()
+                wait(send_sem.at[slot], whole)
+            continue
+
+        longer = down & late
+        passes = relays.get(slot, jnp.bool_(False))
+
+        @pl.when(longer & passes)
+        def _():
+            wait(send_sem.at[slot], whole - skipped + rows + BLK)
+
+        @pl.when(longer & jnp.logical_not(passes))
+        def _():
+            wait(send_sem.at[slot], whole - skipped + rows)
+
+        plain = jnp.logical_not(longer)
+
+        @pl.when(plain if sends is None else plain & sends)
+        def _():
+            wait(send_sem.at[slot], whole)
 
 
 def finish(done_ref, acc_ref, weights_ref, share_ref, recv_ref, out_hbm, last_ref, sem):
@@ -430,9 +414,6 @@
     clip_count, slab_count, band_count = (lax.axis_size(axis) for axis in ("clip", "tm", "band"))
     sources = (2 if slab_count > 1 else 0) + min(band_count - 1, 2)
     assert rows == 2 * BLK and adj_mask.shape[3] == 2 and border_blocks.shape[3] == 1
-    pieces = len(ahead_parts(heads))
-    block_sems = pltpu.SemaphoreType.DMA((sources, 2, len(value_chunks(heads))))
-    ahead_sems = pltpu.SemaphoreType.DMA((sources, pieces + 1))
     last = last_heads(heads)
     parts = pl.pallas_call(
         functools.partial(kernel, clip_count, slab_count, band_count),
@@ -446,35 +427,29 @@
         in_specs=[pl.BlockSpec(memory_space=pl.ANY)] * 5,
         out_specs=[pl.BlockSpec(memory_space=pltpu.VMEM)] * 5,
         scratch_shapes=[
-            pltpu.VMEM((rows, width), jnp.bfloat16),
-            pltpu.VMEM((rows // BLK, BLK, width), jnp.bfloat16),
+            pltpu.VMEM((2 * rows // BLK, BLK, width), jnp.bfloat16),
             pltpu.VMEM((rows // BLK, BLK, width), jnp.bfloat16),
             pltpu.SMEM(adj_mask.shape[2:], jnp.int32),
             pltpu.SMEM(border_blocks.shape[:1:-1], jnp.int32),
-            pltpu.VMEM((sources, 2, heads * BLK, HD), jnp.bfloat16),
+            pltpu.VMEM(((sources + 1) * 2 * heads * BLK, HD), jnp.bfloat16),
             pltpu.VMEM((sources, 2, heads * BLK, HD), jnp.bfloat16),
             pltpu.VMEM((heads, rows, HD), jnp.float32),
             pltpu.VMEM((heads, rows, sources * BLK), jnp.bfloat16),
             pltpu.VMEM((heads, rows, HD), jnp.float32),
-            pltpu.VMEM((sources, pieces, rows // BLK, BLK, HD), jnp.bfloat16),
+            pltpu.VMEM((sources, rows // BLK, BLK, HD), jnp.bfloat16),
             pltpu.VMEM((sources, BLK, HD), jnp.bfloat16),
-            pltpu.SMEM(adj_mask.shape[2:], jnp.int32),
-            pltpu.SMEM(border_blocks.shape[:1:-1], jnp.int32),
-            pltpu.SemaphoreType.DMA((5,)),
-            pltpu.SemaphoreType.REGULAR((max(1, (slab_count > 1) + (band_count > 1) + (clip_count > 1)),)),
-            block_sems,
-            block_sems,
-            ahead_sems,
-            ahead_sems,
+            pltpu.SemaphoreType.DMA((4,)),
+            pltpu.SemaphoreType.REGULAR,
             pltpu.SemaphoreType.DMA((sources,)),
+            pltpu.SemaphoreType.DMA,
+            pltpu.SemaphoreType.DMA,
             pltpu.SemaphoreType.DMA((sources,)),
-            pltpu.SemaphoreType.DMA((sources,)),
-            pltpu.SemaphoreType.DMA((sources,)),
+            pltpu.SemaphoreType.DMA((2,)),
         ],
         compiler_params=pltpu.CompilerParams(collective_id=0, has_side_effects=True),
         name="radial_attention",
     )(
-        queries[0, 0],
+        queries.reshape(rows // BLK, BLK, width),
         keys.reshape(rows // BLK, BLK, width),
         values.reshape(rows // BLK, BLK, width),
         adj_mask[0, 0], border_blocks[0, 0].T,

time: 13.4 us -> 13.1 us (0.978)
  Pallas kernels: 13.3 us -> 12.9 us
    pallas_call x1, Pallas kernels: 12.4 us -> 12.1 us  [per_device(): pl.pallas_call(functools.partial(kernel, clip_count, slab_count, band_cou...]
where the time goes in v5:
time: 13.1 us; the launch traced here: 13 us
  Pallas kernels  12.9 us (98%)
    pallas_call x1, Pallas kernels, per_device(): pl.pallas_call(functools.partial(kernel, clip_count, slab_count, band_cou...  12.1 us
    pallas_call x1, Pallas kernels, per_device(): pl.pallas_call(finish, out_shape=jax.ShapeDtypeStruct((rows, width), jnp....  0.85 us

profile of v5, /device:TPU:1, one launch (start us, length us, event | category | flops | bytes accessed | tf_op | source)
XLA Modules:
  0.0 13.0 jit_solution(3598780082597139142)
XLA Ops:
  0.0 12.1 %radial_attention.1 = (bf16[256,640]{1,0:T(8,128)(2,1)S(1)}, f32[1,256,128]{2,1,0:T(8,128)S(1)}, bf16[1,256,384]{2,1,0:T(8,128)(2,1)S(1)}, f32[1,256,128]{2,1,0:T(8,128)S(1)}, bf16[3,128,128]{2,1,0:T(8,128)(2,1)S(1)}) custom-call(bf16[2,128,768]{2,1,0:T(8,128)(2,1)} %bitcast.6, bf16[2,128,768]{2,1,0:T(8,128)(2,1)} %bitcast.7, bf16[2,128,768]{2,1,0:T(8,128)(2,1)} %bitcast.8, ...), custom_call_target="tpu_custom_call" | custom-call | tf_op jit(solution)/shard_map/radial_attention/pallas_call | solution.py:418
  12.1 0.8 %last_heads.1 = bf16[256,768]{1,0:T(8,128)(2,1)} custom-call(bf16[256,640]{1,0:T(8,128)(2,1)S(1)} %get-tuple-element.10.done_ref, f32[1,256,128]{2,1,0:T(8,128)S(1)} %get-tuple-element.11.acc_ref, bf16[1,256,384]{2,1,0:T(8,128)(2,1)S(1)} %get-tuple-element.12.weights_ref, f32[1,256,128]{2,1,0:T(8,128)S(1)} %get-tuple-element.13.share_ref, ...), custom_call_target="tpu_custom_call" | custom-call | tf_op jit(solution)/shard_map/last_heads/pallas_call | solution.py:457

commit v6 on v5

--- a/solution.py
+++ b/solution.py
@@ -60,7 +60,7 @@
 
 def kernel(
     clip_count, slab_count, band_count, q_hbm, k_hbm, v_hbm, adj_hbm, border_hbm,
-    out_ref, last_acc_ref, last_weights_ref, last_share_ref, last_recv_ref,
+    out_ref, last_acc_ref, last_weights_ref, last_share_ref, values_ref,
     vq_ref, k_ref, adj_ref, border_ref, send_ref, recv_ref, acc_ref, weights_ref, share_ref,
     both_ref, pass_ref,
     load_sem, here_sem, send_sem, ahead_sem, pass_sem, key_sem, value_sem,
@@ -94,6 +94,12 @@
     lends = {slot: at(*source) for slot, (source, _) in detours.items()}
     relays = {slot: at(*middle) for slot, (_, middle) in detours.items()}
 
+    owns = [slot for slot, (*_, above) in enumerate(plan) if above is not None]
+    takes = [slot for slot, (*_, above) in enumerate(plan) if above is None]
+
+    def sent(slot):
+        return send_sem.at[owns.index(slot)] if slot in owns else load_sem.at[takes.index(slot)]
+
     def base(slot, part):
         return (slot * 2 + part) * heads * BLK
 
@@ -101,7 +107,7 @@
         return pltpu.make_async_remote_copy(
             src_ref=send_ref.at[pl.ds(base(slot, 1), BLK)],
             dst_ref=pass_ref.at[slot],
-            send_sem=send_sem.at[slot],
+            send_sem=sent(slot),
             recv_sem=pass_sem,
             device_id=dict(zip(("clip", "tm", "band"), detours[slot][1])),
             device_id_type=MESH,
@@ -110,8 +116,8 @@
     def relay(slot):
         return pltpu.make_async_remote_copy(
             src_ref=pass_ref.at[slot],
-            dst_ref=recv_ref.at[slot, 1, pl.ds(0, BLK)],
-            send_sem=send_sem.at[slot],
+            dst_ref=values_ref.at[slot, pl.ds(0, BLK)],
+            send_sem=sent(slot),
             recv_sem=value_sem.at[0],
             device_id={"clip": 0, "tm": 0, "band": 0},
             device_id_type=MESH,
@@ -138,13 +144,13 @@
     chunks = [[(0, heads * BLK)], value_chunks(heads)]
     skipped = BLK - FLAG
 
-    def transfer(slot, part, group, skip=0):
-        start, size = chunks[part][group]
+    def transfer(slot, part, group, skip=0, whole=False):
+        start, size = (0, heads * BLK) if whole else chunks[part][group]
         at = pl.ds(start + skip, size - skip)
         return pltpu.make_async_remote_copy(
             src_ref=send_ref.at[pl.ds(base(slot, part) + start + skip, size - skip)],
-            dst_ref=last_recv_ref.at[slot] if group else recv_ref.at[slot, part, at],
-            send_sem=send_sem.at[slot],
+            dst_ref=values_ref.at[slot, at] if part else recv_ref.at[slot, at],
+            send_sem=sent(slot),
             recv_sem=value_sem.at[group] if part else key_sem.at[slot],
             device_id=plan[slot][0],
             device_id_type=MESH,
@@ -154,7 +160,7 @@
         return pltpu.make_async_remote_copy(
             src_ref=k_hbm.at[:, :, pl.ds(0, HD)],
             dst_ref=both_ref.at[slot],
-            send_sem=send_sem.at[slot],
+            send_sem=sent(slot),
             recv_sem=ahead_sem,
             device_id=plan[slot][0],
             device_id_type=MESH,
@@ -264,14 +270,17 @@
             send(slot, 1, True)
             send(slot, 1, False)
 
-    pl.when(early)(send_values)
+    for slot, (_, up, down, _, _, _) in enumerate(plan):
+        @pl.when(early & (down if up is None else up if down is None else up | down))
+        def _():
+            transfer(slot, 1, 0, whole=True).start()
 
     for slot, (_, _, _, comes, _, _) in enumerate(plan):
         if comes is not None:
             @pl.when(jnp.logical_not(comes))
             def _():
                 recv_ref[slot] = jnp.zeros(recv_ref.shape[1:], recv_ref.dtype)
-                last_recv_ref[slot] = jnp.zeros(last_recv_ref.shape[1:], recv_ref.dtype)
+                values_ref[slot] = jnp.zeros(values_ref.shape[1:], values_ref.dtype)
 
     first_last = heads - last_acc_ref.shape[0]
 
@@ -306,8 +315,8 @@
             @pl.when(above & late)
             def _():
                 transfer(slot, 0, 0, skipped).wait_recv()
-                flag = recv_ref[slot, 0, skipped:BLK].astype(jnp.float32)
-                recv_ref[slot, 0, :BLK] = jnp.where(
+                flag = recv_ref[slot, skipped:BLK].astype(jnp.float32)
+                recv_ref[slot, :BLK] = jnp.where(
                     jnp.concatenate([flag] * (BLK // FLAG), axis=0) > 0.5,
                     both_ref[slot, 1].astype(jnp.float32),
                     both_ref[slot, 0].astype(jnp.float32),
@@ -327,10 +336,8 @@
 
     pl.when(late)(send_values)
 
-    def arrived(part, head):
-        return jnp.concatenate(
-            [recv_ref[slot, part, head * BLK : (head + 1) * BLK] for slot in slots], axis=0
-        )
+    def arrived(ref, head):
+        return jnp.concatenate([ref[slot, head * BLK : (head + 1) * BLK] for slot in slots], axis=0)
 
     hidden = [
         None if comes is None else jnp.where(comes, 0.0, masked_score).astype(jnp.float32)
@@ -338,7 +345,7 @@
     ]
     for head in range(heads):
         columns = slice(head * HD, (head + 1) * HD)
-        scores = weigh(query(columns), arrived(0, head))
+        scores = weigh(query(columns), arrived(recv_ref, head))
         scores = [
             scores[:, slot * BLK : (slot + 1) * BLK] + (0.0 if hidden[slot] is None else hidden[slot]) for slot in slots
         ]
@@ -355,11 +362,16 @@
         for slot in slots:
             part_ref[:, slot * BLK : (slot + 1) * BLK] = weights[slot].astype(jnp.bfloat16)
 
+    def came(role):
+        return [role if comes is None else role & comes for _, _, _, comes, _, _ in plan]
+
     for group, (start, size) in enumerate(chunks[1]):
-        wait_for([comes for _, _, _, comes, _, _ in plan], value_sem.at[group], size)
+        if group == 0:
+            wait_for(came(early), value_sem.at[group], heads * BLK)
+        wait_for(came(late), value_sem.at[group], size)
         for head in range(start // BLK, min((start + size) // BLK, first_last)):
             result = acc_ref[head] + jnp.dot(
-                weights_ref[head], arrived(1, head), preferred_element_type=jnp.float32
+                weights_ref[head], arrived(values_ref, head), preferred_element_type=jnp.float32
             )
             out_ref[:, head * HD : (head + 1) * HD] = (result * share_ref[head]).astype(out_ref.dtype)
 
@@ -369,7 +381,7 @@
         if above is None:
             @when(sends)
             def _():
-                wait(send_sem.at[slot], whole)
+                wait(sent(slot), whole)
             continue
 
         longer = down & late
@@ -377,35 +389,35 @@
 
         @pl.when(longer & passes)
         def _():
-            wait(send_sem.at[slot], whole - skipped + rows + BLK)
+            wait(sent(slot), whole - skipped + rows + BLK)
 
         @pl.when(longer & jnp.logical_not(passes))
         def _():
-            wait(send_sem.at[slot], whole - skipped + rows)
+            wait(sent(slot), whole - skipped + rows)
 
         plain = jnp.logical_not(longer)
 
         @pl.when(plain if sends is None else plain & sends)
         def _():
-            wait(send_sem.at[slot], whole)
-
-
-def finish(done_ref, acc_ref, weights_ref, share_ref, recv_ref, out_hbm, last_ref, sem):
+            wait(sent(slot), whole)
+
+
+def finish(done_ref, acc_ref, weights_ref, share_ref, values_ref, out_hbm, last_ref, sem):
     width = done_ref.shape[1]
-    copies = [
-        pltpu.make_async_copy(done_ref, out_hbm.at[:, pl.ds(0, width)], sem.at[0]),
-        pltpu.make_async_copy(last_ref, out_hbm.at[:, pl.ds(width, last_ref.shape[1])], sem.at[1]),
-    ]
-    copies[0].start()
+    first = width // HD
+    pltpu.make_async_copy(done_ref, out_hbm.at[:, pl.ds(0, width)], sem).start()
     for head in range(acc_ref.shape[0]):
         values = jnp.concatenate(
-            [recv_ref[slot, head * BLK : (head + 1) * BLK] for slot in range(recv_ref.shape[0])], axis=0
+            [
+                values_ref[slot, (first + head) * BLK : (first + head + 1) * BLK]
+                for slot in range(values_ref.shape[0])
+            ],
+            axis=0,
         )
         result = acc_ref[head] + jnp.dot(weights_ref[head], values, preferred_element_type=jnp.float32)
         last_ref[:, head * HD : (head + 1) * HD] = (result * share_ref[head]).astype(last_ref.dtype)
-    copies[1].start()
-    for copy in copies:
-        copy.wait()
+    pltpu.make_async_copy(last_ref, out_hbm.at[:, pl.ds(width, last_ref.shape[1])], sem).start()
+    pltpu.make_async_copy(out_hbm, out_hbm, sem).wait()
 
 
 def per_device(queries, keys, values, adj_mask, border_blocks):
@@ -422,7 +434,7 @@
             pltpu.VMEM((last, rows, HD), jnp.float32),
             pltpu.VMEM((last, rows, sources * BLK), jnp.bfloat16),
             pltpu.VMEM((last, rows, HD), jnp.float32),
-            pltpu.VMEM((sources, last * BLK, HD), jnp.bfloat16),
+            pltpu.VMEM((sources, heads * BLK, HD), jnp.bfloat16),
         ],
         in_specs=[pl.BlockSpec(memory_space=pl.ANY)] * 5,
         out_specs=[pl.BlockSpec(memory_space=pltpu.VMEM)] * 5,
@@ -432,7 +444,7 @@
             pltpu.SMEM(adj_mask.shape[2:], jnp.int32),
             pltpu.SMEM(border_blocks.shape[:1:-1], jnp.int32),
             pltpu.VMEM(((sources + 1) * 2 * heads * BLK, HD), jnp.bfloat16),
-            pltpu.VMEM((sources, 2, heads * BLK, HD), jnp.bfloat16),
+            pltpu.VMEM((sources, heads * BLK, HD), jnp.bfloat16),
             pltpu.VMEM((heads, rows, HD), jnp.float32),
             pltpu.VMEM((heads, rows, sources * BLK), jnp.bfloat16),
             pltpu.VMEM((heads, rows, HD), jnp.float32),
@@ -440,7 +452,7 @@
             pltpu.VMEM((sources, BLK, HD), jnp.bfloat16),
             pltpu.SemaphoreType.DMA((4,)),
             pltpu.SemaphoreType.REGULAR,
-            pltpu.SemaphoreType.DMA((sources,)),
+            pltpu.SemaphoreType.DMA(((slab_count > 1) + (band_count > 1),)),
             pltpu.SemaphoreType.DMA,
             pltpu.SemaphoreType.DMA,
             pltpu.SemaphoreType.DMA((sources,)),
@@ -459,7 +471,7 @@
         out_shape=jax.ShapeDtypeStruct((rows, width), jnp.bfloat16),
         in_specs=[pl.BlockSpec(memory_space=pltpu.VMEM)] * 5,
         out_specs=pl.BlockSpec(memory_space=pl.ANY),
-        scratch_shapes=[pltpu.VMEM((rows, last * HD), jnp.bfloat16), pltpu.SemaphoreType.DMA((2,))],
+        scratch_shapes=[pltpu.VMEM((rows, last * HD), jnp.bfloat16), pltpu.SemaphoreType.DMA],
         name="last_heads",
     )(*(pltpu.with_memory_space_constraint(part, pltpu.VMEM) for part in parts))
     return attended[None, None]

time: 13.1 us -> 13.1 us (level)
  no operation moved by 1% of the time
where the time goes in v6:
time: 13.1 us; the launch traced here: 12.9 us
  Pallas kernels  12.9 us (98%)
    pallas_call x1, Pallas kernels, per_device(): pl.pallas_call(functools.partial(kernel, clip_count, slab_count, band_cou...  12.1 us
    pallas_call x1, Pallas kernels, per_device(): pl.pallas_call(finish, out_shape=jax.ShapeDtypeStruct((rows, width), jnp....  0.84 us

profile of v6, /device:TPU:1, one launch (start us, length us, event | category | flops | bytes accessed | tf_op | source)
XLA Modules:
  0.0 12.9 jit_solution(18040111288719856722)
XLA Ops:
  0.0 12.1 %radial_attention.1 = (bf16[256,640]{1,0:T(8,128)(2,1)S(1)}, f32[1,256,128]{2,1,0:T(8,128)S(1)}, bf16[1,256,384]{2,1,0:T(8,128)(2,1)S(1)}, f32[1,256,128]{2,1,0:T(8,128)S(1)}, bf16[3,768,128]{2,1,0:T(8,128)(2,1)S(1)}) custom-call(bf16[2,128,768]{2,1,0:T(8,128)(2,1)} %bitcast.6, bf16[2,128,768]{2,1,0:T(8,128)(2,1)} %bitcast.7, bf16[2,128,768]{2,1,0:T(8,128)(2,1)} %bitcast.8, ...), custom_call_target="tpu_custom_call" | custom-call | tf_op jit(solution)/shard_map/radial_attention/pallas_call | solution.py:430
  12.1 0.8 %last_heads.1 = bf16[256,768]{1,0:T(8,128)(2,1)} custom-call(bf16[256,640]{1,0:T(8,128)(2,1)S(1)} %get-tuple-element.10.done_ref, f32[1,256,128]{2,1,0:T(8,128)S(1)} %get-tuple-element.11.acc_ref, bf16[1,256,384]{2,1,0:T(8,128)(2,1)S(1)} %get-tuple-element.12.weights_ref, f32[1,256,128]{2,1,0:T(8,128)S(1)} %get-tuple-element.13.share_ref, ...), custom_call_target="tpu_custom_call" | custom-call | tf_op jit(solution)/shard_map/last_heads/pallas_call | solution.py:469
